TPU v7x, 32 devices: a whole 2x2x4 slice. The times are simulated.
32 devices in a mesh: groups: 2 (over y), frame: 4 (over z), quarter: 2 (over x), sub: 2 (over core).
Axes of the slice: x: 2, y: 2, z: 4, core: 2. Of those that a mesh axis runs over, the one named last changes fastest.
Arguments:
- queries: bfloat16 [16, 1024, 256], P(('groups', 'frame'), ('quarter', 'sub')), parts along dimension 0, may hold values from -36 to 36
- keys: bfloat16 [16, 1024, 256], P(('groups', 'frame'), ('quarter', 'sub')), parts along dimension 0, may hold values from -6 to 6
- values: bfloat16 [16, 1024, 256], P(('groups', 'frame'), ('quarter', 'sub')), parts along dimension 0, may hold values from -6 to 6
Outputs:
- attended: bfloat16 [16, 1024, 256], P(('groups', 'frame'), ('quarter', 'sub')), parts along dimension 0
There are 2 independent parts, one for each index of `groups`. A program takes and returns all parts, laid end to end along the dimension named above; each array names one. Nothing has to cross between parts.
All inputs are finite; a program needn't handle non-finite values.
Results may differ from a plain program's by a relative error of at most 0.0028.
Values may be sent and summed in bfloat16 or wider, within the bound.
A program may use at most 64 MiB of HBM per device.

v0:
```python
import math
import jax
import jax.numpy as jnp
from jax import lax
from jax.sharding import PartitionSpec as P

STRIP = 16


def partial_attend(query_rows, key_rows, value_rows, running, score_scale):
    top_run, sum_run, acc_run = running
    scores = (
        jnp.einsum("frd,fnd->frn", query_rows, key_rows, preferred_element_type=jnp.float32)
        * score_scale
    )
    highest = jnp.maximum(top_run, jnp.max(scores, axis=-1, keepdims=True))
    expo = jnp.exp(scores - highest)
    factor = jnp.exp(top_run - highest)
    sum_next = sum_run * factor + jnp.sum(expo, axis=-1, keepdims=True)
    acc_next = acc_run * factor + jnp.einsum(
        "frn,fnd->frd", expo.astype(jnp.bfloat16), value_rows, preferred_element_type=jnp.float32
    )
    return (highest, sum_next, acc_next)


def fold_keys(query_rows, score_scale, running, pieces):
    key_piece, value_piece = pieces
    length = key_piece.shape[1]
    block_keys = math.gcd(length, 2048)
    for block_index in range(length // block_keys):
        lower = block_index * block_keys
        running = partial_attend(
            query_rows,
            key_piece[:, lower : lower + block_keys],
            value_piece[:, lower : lower + block_keys],
            running,
            score_scale,
        )
    return running


def empty_state(query_rows):
    frames_here, rows_here, width = query_rows.shape
    return (
        jnp.full((frames_here, rows_here, 1), -jnp.inf, jnp.float32),
        jnp.zeros((frames_here, rows_here, 1), jnp.float32),
        jnp.zeros((frames_here, rows_here, width), jnp.float32),
    )


def body(queries, keys, values):
    head_width = queries.shape[2] // 2
    frames_dev = queries.shape[0]
    tokens_dev = queries.shape[1]
    score_scale = 1.0 / math.sqrt(head_width)
    query_spatial = queries[:, :, :head_width]
    key_spatial = keys[:, :, :head_width]
    value_spatial = values[:, :, :head_width]
    frame_count = lax.axis_size("frame")
    local_strips = tokens_dev // (STRIP * frame_count)

    def to_strips(array):
        part_two = array[:, :, head_width:].reshape(
            frames_dev, frame_count, local_strips, STRIP, head_width
        )
        return part_two.transpose(1, 2, 0, 3, 4)

    query_strip = lax.all_to_all(
        to_strips(queries), "frame", split_axis=0, concat_axis=2, tiled=True
    )
    key_strip = lax.all_to_all(to_strips(keys), "frame", split_axis=0, concat_axis=2, tiled=True)
    value_strip = lax.all_to_all(
        to_strips(values), "frame", split_axis=0, concat_axis=2, tiled=True
    )
    item_count = query_strip.shape[1]
    frames_all = query_strip.shape[2]
    rows_strip = frames_all * STRIP
    query_flat = query_strip.reshape(item_count, rows_strip, head_width)
    key_flat = key_strip.reshape(item_count, rows_strip, head_width)
    value_flat = value_strip.reshape(item_count, rows_strip, head_width)
    scores = (
        jnp.einsum("nqd,nkd->nqk", query_flat, key_flat, preferred_element_type=jnp.float32)
        * score_scale
    )
    highest = jnp.max(scores, axis=-1, keepdims=True)
    expo = jnp.exp(scores - highest)
    totals = jnp.sum(expo, axis=-1, keepdims=True)
    mixed = jnp.einsum(
        "nqk,nkd->nqd", expo.astype(jnp.bfloat16), value_flat, preferred_element_type=jnp.float32
    )
    strip_out = (
        (mixed / totals).astype(jnp.bfloat16).reshape(1, item_count, frames_all, STRIP, head_width)
    )
    returned = lax.all_to_all(strip_out, "frame", split_axis=2, concat_axis=0, tiled=True)
    temporal = returned.transpose(2, 0, 1, 3, 4).reshape(frames_dev, tokens_dev, head_width)
    top_all, total_spatial, acc_spatial = fold_keys(
        query_spatial,
        score_scale,
        empty_state(query_spatial),
        (
            lax.all_gather(key_spatial, ("quarter", "sub"), axis=1, tiled=True),
            lax.all_gather(value_spatial, ("quarter", "sub"), axis=1, tiled=True),
        ),
    )
    spatial = (acc_spatial / total_spatial).astype(jnp.bfloat16)
    return jnp.concatenate([spatial, temporal], axis=-1)


def solution(mesh):
    in_specs = (
        P(("groups", "frame"), ("quarter", "sub"), None),
        P(("groups", "frame"), ("quarter", "sub"), None),
        P(("groups", "frame"), ("quarter", "sub"), None),
    )
    out_specs = P(("groups", "frame"), ("quarter", "sub"), None)
    return jax.shard_map(body, mesh=mesh, in_specs=in_specs, out_specs=out_specs, check_vma=False)
```

profile of v0, /device:TPU:0, one launch (start us, length us, event | category | flops | bytes accessed | tf_op | source)
XLA Modules:
  0.0 53.8 jit_solution(1499810248122373728)
XLA Ops:
  0.0 1.0 %fusion.16 = (bf16[2,256,128]{2,1,0:T(8,128)(2,1)S(1)}, bf16[2,256,128]{2,1,0:T(8,128)(2,1)S(1)}) fusion(bf16[2,256,256]{2,1,0:T(8,128)(2,1)} %param.4), kind=kLoop, calls=%fused_computation.22 | loop fusion | bytes 524288 | tf_op jit(solution)/shard_map/slice | solution.py:57
  1.0 0.0 copy-start
  1.0 0.7 %copy.31 = bf16[4,4,2,16,128]{4,3,2,1,0:T(8,128)(2,1)} copy(bf16[4,4,2,16,128]{4,3,1,0,2:T(8,128)(2,1)S(1)} %bitcast.42) | data formatting | bytes 262144 | tf_op jit(solution)/shard_map/transpose | solution.py:66
  1.7 6.3 %all-to-all-start.1 = ((bf16[4,4,2,16,128]{4,3,2,1,0:T(8,128)(2,1)}), bf16[4,4,2,16,128]{4,3,2,1,0:T(8,128)(2,1)S(1)}, u32[]{:S(2)}, u32[]{:S(2)}) async-start(bf16[4,4,2,16,128]{4,3,2,1,0:T(8,128)(2,1)} %copy.31), calls=%async_computation.1 | async-start | bytes 262144 | tf_op jit(solution)/shard_map/all_to_all | solution.py:71
  8.0 0.0 slice-start
  8.0 7.3 %all_gather.6 = bf16[2,1024,128]{2,1,0:T(8,128)(2,1)S(1)} all-gather(bf16[2,256,128]{2,1,0:T(8,128)(2,1)S(1)} %get-tuple-element.5), channel_id=1, replica_groups=mesh['groups'=2,'frame'=4,'quarter'=2,'sub'=2] {'quarter','sub'}, dimensions={1}, use_global_device_ids=true | all-gather | bytes 655360 | tf_op jit(solution)/shard_map/all_gather | solution.py:101
  15.3 1.4 %multiply_reduce_fusion = (f32[2,256]{1,0:T(2,128)S(1)}, f32[2,256,1024]{2,1,0:T(8,128)S(1)}) fusion(bf16[2,1024,128]{2,1,0:T(8,128)(2,1)S(1)} %all_gather.6, bf16[2,256,256]{2,1,0:T(8,128)(2,1)} %param.3), kind=kOutput, calls=%fused_computation.1 | convolution fusion | flops 135265792 | bytes 2754560 | tf_op jit(solution)/shard_map/frd,fnd->frn/dot_general | solution.py:13
  16.7 0.0 copy-done
  16.8 0.1 copy.43
  16.9 0.0 slice-done
  16.9 0.7 %copy.29 = bf16[4,4,2,16,128]{4,3,2,1,0:T(8,128)(2,1)} copy(bf16[4,4,2,16,128]{4,3,1,0,2:T(8,128)(2,1)S(1)} %bitcast.37) | data formatting | bytes 262144 | tf_op jit(solution)/shard_map/transpose | solution.py:66
  17.6 0.7 %copy.33 = bf16[4,4,2,16,128]{4,3,2,1,0:T(8,128)(2,1)} copy(bf16[4,4,2,16,128]{4,3,1,0,2:T(8,128)(2,1)S(1)} %bitcast.41) | data formatting | bytes 262144 | tf_op jit(solution)/shard_map/transpose | solution.py:66
  18.2 0.5 fusion
  18.7 0.0 all-to-all-done.1
  18.7 5.1 %all-to-all-start = ((bf16[4,4,2,16,128]{4,3,2,1,0:T(8,128)(2,1)}), bf16[4,4,2,16,128]{4,3,2,1,0:T(8,128)(2,1)S(1)}, u32[]{:S(2)}, u32[]{:S(2)}) async-start(bf16[4,4,2,16,128]{4,3,2,1,0:T(8,128)(2,1)} %copy.29), calls=%async_computation | async-start | bytes 262144 | tf_op jit(solution)/shard_map/all_to_all | solution.py:68
  23.9 6.4 %all-to-all-done = bf16[4,4,2,16,128]{4,3,2,1,0:T(8,128)(2,1)S(1)} async-done(((bf16[4,4,2,16,128]{4,3,2,1,0:T(8,128)(2,1)}), bf16[4,4,2,16,128]{4,3,2,1,0:T(8,128)(2,1)S(1)}, u32[]{:S(2)}, u32[]{:S(2)}) %all-to-all-start) | async-done | bytes 131104 | tf_op jit(solution)/shard_map/all_to_all | solution.py:68
  30.3 3.3 %all-to-all-start.2 = ((bf16[4,4,2,16,128]{4,3,2,1,0:T(8,128)(2,1)}), bf16[4,4,2,16,128]{4,3,2,1,0:T(8,128)(2,1)S(1)}, u32[]{:S(2)}, u32[]{:S(2)}) async-start(bf16[4,4,2,16,128]{4,3,2,1,0:T(8,128)(2,1)} %copy.33), calls=%async_computation.2 | async-start | bytes 262144 | tf_op jit(solution)/shard_map/all_to_all | solution.py:72
  33.6 6.5 %all_gather.7 = bf16[2,1024,128]{1,2,0:T(8,128)(2,1)S(1)} all-gather(bf16[2,256,128]{1,2,0:T(8,128)(2,1)S(1)} %copy.43), channel_id=1, replica_groups=mesh['groups'=2,'frame'=4,'quarter'=2,'sub'=2] {'quarter','sub'}, dimensions={1}, use_global_device_ids=true | all-gather | bytes 655360 | tf_op jit(solution)/shard_map/all_gather | solution.py:102
  40.1 0.0 all-to-all-done.2
  40.2 0.2 fusion.18
  40.4 0.1 fusion.8
  40.5 0.3 fusion.3
  40.7 0.7 %copy.36 = bf16[1,4,8,16,128]{4,3,1,0,2:T(8,128)(2,1)} copy(bf16[1,4,8,16,128]{4,3,2,1,0:T(8,128)(2,1)S(1)} %bitcast.44) | data formatting | bytes 262144 | tf_op jit(solution)/shard_map/reshape | solution.py:92
  41.4 5.0 %all-to-all-start.3 = ((bf16[1,4,8,16,128]{4,3,1,0,2:T(8,128)(2,1)}), bf16[1,4,8,16,128]{4,3,1,0,2:T(8,128)(2,1)S(1)}, u32[]{:S(2)}, u32[]{:S(2)}) async-start(bf16[1,4,8,16,128]{4,3,1,0,2:T(8,128)(2,1)} %copy.36), calls=%async_computation.3 | async-start | bytes 262144 | tf_op jit(solution)/shard_map/all_to_all | solution.py:94
  46.4 0.6 %fusion.4 = bf16[2,256,128]{1,2,0:T(8,128)(2,1)S(1)} fusion(bf16[2,1024,128]{1,2,0:T(8,128)(2,1)S(1)} %all_gather.7, f32[2,256,1024]{2,1,0:T(8,128)S(1)} %get-tuple-element.14, f32[2,256]{1,0:T(2,128)S(1)} %get-tuple-element.13, f32[2,256]{1,0:T(2,128)S(1)} %get-tuple-element.10, f32[2,256]{1,0:T(2,128)S(1)} %get-tuple-element.9), kind=kOutput, calls=%fused_computation.9 | convolution fusion | flops 135987200 | bytes 2758656 | tf_op jit(solution)/shard_map/frn,fnd->frd/dot_general | solution.py:20
  47.0 5.8 %all-to-all-done.3 = bf16[1,4,8,16,128]{4,3,1,0,2:T(8,128)(2,1)S(1)} async-done(((bf16[1,4,8,16,128]{4,3,1,0,2:T(8,128)(2,1)}), bf16[1,4,8,16,128]{4,3,1,0,2:T(8,128)(2,1)S(1)}, u32[]{:S(2)}, u32[]{:S(2)}) %all-to-all-start.3) | async-done | bytes 131104 | tf_op jit(solution)/shard_map/all_to_all | solution.py:94
  52.9 0.1 copy.39
  53.0 0.8 %copy.40 = bf16[2,256,256]{2,1,0:T(8,128)(2,1)} copy(bf16[2,256,256]{1,2,0:T(8,128)(2,1)S(1)} %pad_maximum_fusion) | data formatting | bytes 524288 | tf_op jit(solution)/shard_map/concatenate | solution.py:106
  (7 shorter events, 0.1 us)
Async XLA Ops:
  1.0 15.7 %copy-start = (bf16[2,256,256]{2,1,0:T(8,128)(2,1)S(1)}, bf16[2,256,256]{2,1,0:T(8,128)(2,1)}, u32[]{:S(2)}) copy-start(bf16[2,256,256]{2,1,0:T(8,128)(2,1)} %param.5) | copy-start | bytes 786436
  1.7 17.1 %all-to-all-start.1 = ((bf16[4,4,2,16,128]{4,3,2,1,0:T(8,128)(2,1)}), bf16[4,4,2,16,128]{4,3,2,1,0:T(8,128)(2,1)S(1)}, u32[]{:S(2)}, u32[]{:S(2)}) async-start(bf16[4,4,2,16,128]{4,3,2,1,0:T(8,128)(2,1)} %copy.31), calls=%async_computation.1 | async-start | bytes 262144 | tf_op jit(solution)/shard_map/all_to_all | solution.py:71
  8.0 8.9 %slice-start = ((bf16[2,256,256]{2,1,0:T(8,128)(2,1)}), bf16[2,256,128]{2,1,0:T(8,128)(2,1)S(1)}, s32[]{:S(2)}) async-start(bf16[2,256,256]{2,1,0:T(8,128)(2,1)} %param.3), calls=%async_computation.4 | async-start | bytes 262144 | tf_op jit(solution)/shard_map/slice | solution.py:63
  18.7 11.5 %all-to-all-start = ((bf16[4,4,2,16,128]{4,3,2,1,0:T(8,128)(2,1)}), bf16[4,4,2,16,128]{4,3,2,1,0:T(8,128)(2,1)S(1)}, u32[]{:S(2)}, u32[]{:S(2)}) async-start(bf16[4,4,2,16,128]{4,3,2,1,0:T(8,128)(2,1)} %copy.29), calls=%async_computation | async-start | bytes 262144 | tf_op jit(solution)/shard_map/all_to_all | solution.py:68
  30.3 9.9 %all-to-all-start.2 = ((bf16[4,4,2,16,128]{4,3,2,1,0:T(8,128)(2,1)}), bf16[4,4,2,16,128]{4,3,2,1,0:T(8,128)(2,1)S(1)}, u32[]{:S(2)}, u32[]{:S(2)}) async-start(bf16[4,4,2,16,128]{4,3,2,1,0:T(8,128)(2,1)} %copy.33), calls=%async_computation.2 | async-start | bytes 262144 | tf_op jit(solution)/shard_map/all_to_all | solution.py:72
  41.4 11.5 %all-to-all-start.3 = ((bf16[1,4,8,16,128]{4,3,1,0,2:T(8,128)(2,1)}), bf16[1,4,8,16,128]{4,3,1,0,2:T(8,128)(2,1)S(1)}, u32[]{:S(2)}, u32[]{:S(2)}) async-start(bf16[1,4,8,16,128]{4,3,1,0,2:T(8,128)(2,1)} %copy.36), calls=%async_computation.3 | async-start | bytes 262144 | tf_op jit(solution)/shard_map/all_to_all | solution.py:94
where the time goes:
time: 54.4 us; the launch traced here: 53.8 us
  starting transfers between devices  19.8 us (36%)
  blocking collectives  13.8 us (25%)
  waiting for transfers between devices  12.2 us (22%)
  local copies, waits for them, and re-layouts  4.8 us (9%)
  matrix products  2.5 us (5%)
  other arithmetic  0.58 us (1%)
    all_gather x1, blocking collectives, body(): lax.all_gather(key_spatial, ('quarter', 'sub'), axis=1, tiled=True)  7.29 us
    all_gather x1, blocking collectives, body(): lax.all_gather(value_spatial, ('quarter', 'sub'), axis=1, tiled=True)  6.5 us
    all_to_all x1, waiting for transfers between devices, body(): lax.all_to_all(to_strips(queries), 'frame', split_axis=0, concat_axis=2,...  6.41 us
    all_to_all x1, starting transfers between devices, body(): lax.all_to_all(to_strips(keys), 'frame', split_axis=0, concat_axis=2, til...  6.35 us
    all_to_all x1, waiting for transfers between devices, body(): lax.all_to_all(strip_out, 'frame', split_axis=2, concat_axis=0, tiled=True)  5.8 us
    all_to_all x1, starting transfers between devices, body(): lax.all_to_all(to_strips(queries), 'frame', split_axis=0, concat_axis=2,...  5.1 us
    all_to_all x1, starting transfers between devices, body(): lax.all_to_all(strip_out, 'frame', split_axis=2, concat_axis=0, tiled=True)  5.04 us
    all_to_all x1, starting transfers between devices, body(): lax.all_to_all(to_strips(values), 'frame', split_axis=0, concat_axis=2, t...  3.33 us
  transfers between devices with their start and end apart: 4, of which 2 were waited for; matrix products, arithmetic and copies ran while one was open for 7% of the time, Pallas kernels for 0%

commit v1 on v0

--- a/solution.py
+++ b/solution.py
@@ -5,6 +5,24 @@
 from jax.sharding import PartitionSpec as P
 
 STRIP = 16
+
+
+def gather_around(shard, axis, dim):
+    ways, here, step = (lax.axis_size(axis), lax.axis_index(axis), shard.shape[dim])
+    shape = [n * ways if d == dim else n for d, n in enumerate(shard.shape)]
+    full = lax.dynamic_update_slice_in_dim(
+        jnp.zeros(shape, shard.dtype), shard, here * step, axis=dim
+    )
+    going_up = going_down = shard
+    for far in range(1, ways // 2 + 1):
+        going_up = lax.ppermute(going_up, axis, [(d, (d + 1) % ways) for d in range(ways)])
+        full = lax.dynamic_update_slice_in_dim(full, going_up, (here - far) % ways * step, axis=dim)
+        if 2 * far < ways:
+            going_down = lax.ppermute(going_down, axis, [(d, (d - 1) % ways) for d in range(ways)])
+            full = lax.dynamic_update_slice_in_dim(
+                full, going_down, (here + far) % ways * step, axis=dim
+            )
+    return full
 
 
 def partial_attend(query_rows, key_rows, value_rows, running, score_scale):
@@ -98,7 +116,7 @@
         score_scale,
         empty_state(query_spatial),
         (
-            lax.all_gather(key_spatial, ("quarter", "sub"), axis=1, tiled=True),
+            gather_around(key_spatial, ("quarter", "sub"), 1),
             lax.all_gather(value_spatial, ("quarter", "sub"), axis=1, tiled=True),
         ),
     )

time: 54.4 us -> 49.2 us (0.904)
  blocking collectives: 13.8 us -> 7.17 us
  local copies, waits for them, and re-layouts: 4.8 us -> 5.96 us
  waiting for transfers between devices: 12.2 us -> 13.3 us
  matrix products: 2.5 us -> 1.43 us
    all_gather x1 -> x0, blocking collectives: 7.29 us -> none  [body(): lax.all_gather(key_spatial, ('quarter', 'sub'), axis=1, tiled=True)]
    all_to_all x1, waiting for transfers between devices: 6.41 us -> 0.01 us  [body(): lax.all_to_all(to_strips(queries), 'frame', split_axis=0, concat_axis=2,...]
    all_to_all x1, waiting for transfers between devices: 0.01 us -> 6.37 us  [body(): lax.all_to_all(to_strips(keys), 'frame', split_axis=0, concat_axis=2, til...]
    all_to_all x1, starting transfers between devices: 3.33 us -> 6.35 us  [body(): lax.all_to_all(to_strips(values), 'frame', split_axis=0, concat_axis=2, t...]
    all_to_all x1, waiting for transfers between devices: 0.01 us -> 2.38 us  [body(): lax.all_to_all(to_strips(values), 'frame', split_axis=0, concat_axis=2, t...]
    ppermute x0 -> x3, starting transfers between devices: none -> 2.14 us  [the longest x1 1.73 us: gather_around(): lax.ppermute(going_down, axis, [(d, (d - 1) % ways) for d in range(ways)])]
    all_to_all x1, starting transfers between devices: 5.1 us -> 3.32 us  [body(): lax.all_to_all(to_strips(queries), 'frame', split_axis=0, concat_axis=2,...]
    all_to_all x1, starting transfers between devices: 5.04 us -> 3.33 us  [body(): lax.all_to_all(strip_out, 'frame', split_axis=2, concat_axis=0, tiled=True)]
  transfers between devices with their start and end apart: 4 -> 7, of which waited for: 2 -> 3; matrix products, arithmetic and copies ran while one was open for 7% -> 11% of each run, Pallas kernels for 0% -> 0%
where the time goes in v1:
time: 49.2 us; the launch traced here: 48.6 us
  starting transfers between devices  20.2 us (41%)
  waiting for transfers between devices  13.3 us (27%)
  blocking collectives  7.17 us (15%)
  local copies, waits for them, and re-layouts  5.96 us (12%)
  matrix products  1.43 us (3%)
    all_gather x1, blocking collectives, body(): lax.all_gather(value_spatial, ('quarter', 'sub'), axis=1, tiled=True)  7.17 us
    all_to_all x1, waiting for transfers between devices, body(): lax.all_to_all(to_strips(keys), 'frame', split_axis=0, concat_axis=2, til...  6.37 us
    all_to_all x1, starting transfers between devices, body(): lax.all_to_all(to_strips(values), 'frame', split_axis=0, concat_axis=2, t...  6.35 us
    all_to_all x1, starting transfers between devices, body(): lax.all_to_all(to_strips(keys), 'frame', split_axis=0, concat_axis=2, til...  5.04 us
    all_to_all x1, waiting for transfers between devices, body(): lax.all_to_all(strip_out, 'frame', split_axis=2, concat_axis=0, tiled=True)  4.49 us
    all_to_all x1, starting transfers between devices, body(): lax.all_to_all(strip_out, 'frame', split_axis=2, concat_axis=0, tiled=True)  3.33 us
    all_to_all x1, starting transfers between devices, body(): lax.all_to_all(to_strips(queries), 'frame', split_axis=0, concat_axis=2,...  3.32 us
    all_to_all x1, waiting for transfers between devices, body(): lax.all_to_all(to_strips(values), 'frame', split_axis=0, concat_axis=2, t...  2.38 us
  transfers between devices with their start and end apart: 7, of which 3 were waited for; matrix products, arithmetic and copies ran while one was open for 11% of the time, Pallas kernels for 0%

profile of v1, /device:TPU:0, one launch (start us, length us, event | category | flops | bytes accessed | tf_op | source)
XLA Modules:
  0.0 48.6 jit_solution(7288028177025399771)
XLA Ops:
  0.0 0.0 slice-start
  0.0 1.0 %fusion.17 = (bf16[2,256,128]{2,1,0:T(8,128)(2,1)S(1)}, bf16[2,256,128]{2,1,0:T(8,128)(2,1)S(1)}) fusion(bf16[2,256,256]{2,1,0:T(8,128)(2,1)} %param.5), kind=kLoop, calls=%fused_computation.26 | loop fusion | bytes 524288 | tf_op jit(solution)/shard_map/slice | solution.py:76
  1.0 0.7 %copy.37 = bf16[4,4,2,16,128]{4,3,2,1,0:T(8,128)(2,1)} copy(bf16[4,4,2,16,128]{4,3,1,0,2:T(8,128)(2,1)S(1)} %bitcast.54) | data formatting | bytes 262144 | tf_op jit(solution)/shard_map/transpose | solution.py:84
  1.7 6.3 %all-to-all-start.2 = ((bf16[4,4,2,16,128]{4,3,2,1,0:T(8,128)(2,1)}), bf16[4,4,2,16,128]{4,3,2,1,0:T(8,128)(2,1)S(1)}, u32[]{:S(2)}, u32[]{:S(2)}) async-start(bf16[4,4,2,16,128]{4,3,2,1,0:T(8,128)(2,1)} %copy.37), calls=%async_computation.2 | async-start | bytes 262144 | tf_op jit(solution)/shard_map/all_to_all | solution.py:90
  8.0 0.1 broadcast_in_dim.7
  8.1 1.0 %fusion.18 = (bf16[2,256,128]{2,1,0:T(8,128)(2,1)S(1)}, bf16[2,1024,128]{2,1,0:T(8,128)(2,1)S(1)}, bf16[2,256,128]{2,1,0:T(8,128)(2,1)S(1)}) fusion(bf16[2,256,256]{2,1,0:T(8,128)(2,1)} %param.4, bf16[2,1024,128]{2,1,0:T(8,128)(2,1)S(1)} %broadcast_in_dim.7, s32[]{:T(128)S(6)} %select_n.27), kind=kLoop, calls=%fused_computation.27 | loop fusion | bytes 655364 | tf_op jit(solution)/shard_map/slice | solution.py:75
  9.1 0.1 collective-permute-start
  9.2 1.7 %collective-permute-start.1 = (bf16[2,256,128]{2,1,0:T(8,128)(2,1)S(1)}, bf16[2,256,128]{2,1,0:T(8,128)(2,1)S(1)}, u32[]{:S(2)}, u32[]{:S(2)}) collective-permute-start(bf16[2,256,128]{2,1,0:T(8,128)(2,1)S(1)} %get-tuple-element.7), channel_id=1, source_target_pairs={{0,3},{1,0},{2,1},{3,2},{4,7},{5,4},{6,5},{7,6},{8,11},{9,8},{10,9... | collective-permute-start | bytes 393224 | tf_op jit(solution)/shard_map/ppermute | solution.py:21
  10.9 0.0 slice-done
  10.9 0.7 %copy.33 = bf16[4,4,2,16,128]{4,3,2,1,0:T(8,128)(2,1)} copy(bf16[4,4,2,16,128]{4,3,1,0,2:T(8,128)(2,1)S(1)} %bitcast.50) | data formatting | bytes 262144 | tf_op jit(solution)/shard_map/transpose | solution.py:84
  11.6 0.1 copy.48
  11.7 2.4 %all-to-all-done.2 = bf16[4,4,2,16,128]{4,3,2,1,0:T(8,128)(2,1)S(1)} async-done(((bf16[4,4,2,16,128]{4,3,2,1,0:T(8,128)(2,1)}), bf16[4,4,2,16,128]{4,3,2,1,0:T(8,128)(2,1)S(1)}, u32[]{:S(2)}, u32[]{:S(2)}) %all-to-all-start.2) | async-done | bytes 131104 | tf_op jit(solution)/shard_map/all_to_all | solution.py:90
  14.1 3.3 %all-to-all-start = ((bf16[4,4,2,16,128]{4,3,2,1,0:T(8,128)(2,1)}), bf16[4,4,2,16,128]{4,3,2,1,0:T(8,128)(2,1)S(1)}, u32[]{:S(2)}, u32[]{:S(2)}) async-start(bf16[4,4,2,16,128]{4,3,2,1,0:T(8,128)(2,1)} %copy.33), calls=%async_computation | async-start | bytes 262144 | tf_op jit(solution)/shard_map/all_to_all | solution.py:86
  17.4 7.2 %all_gather.3 = bf16[2,1024,128]{1,2,0:T(8,128)(2,1)S(1)} all-gather(bf16[2,256,128]{1,2,0:T(8,128)(2,1)S(1)} %copy.48), channel_id=1, replica_groups=mesh['groups'=2,'frame'=4,'quarter'=2,'sub'=2] {'quarter','sub'}, dimensions={1}, use_global_device_ids=true | all-gather | bytes 655360 | tf_op jit(solution)/shard_map/all_gather | solution.py:120
  24.6 0.7 %copy.35 = bf16[4,4,2,16,128]{4,3,2,1,0:T(8,128)(2,1)} copy(bf16[4,4,2,16,128]{4,3,1,0,2:T(8,128)(2,1)S(1)} %bitcast.51) | data formatting | bytes 262144 | tf_op jit(solution)/shard_map/transpose | solution.py:84
  25.3 0.0 copy-start
  25.3 0.0 collective-permute-done
  25.3 0.3 collective-permute-start.2
  25.6 0.0 all-to-all-done
  25.6 5.0 %all-to-all-start.1 = ((bf16[4,4,2,16,128]{4,3,2,1,0:T(8,128)(2,1)}), bf16[4,4,2,16,128]{4,3,2,1,0:T(8,128)(2,1)S(1)}, u32[]{:S(2)}, u32[]{:S(2)}) async-start(bf16[4,4,2,16,128]{4,3,2,1,0:T(8,128)(2,1)} %copy.35), calls=%async_computation.1 | async-start | bytes 262144 | tf_op jit(solution)/shard_map/all_to_all | solution.py:89
  30.7 0.0 collective-permute-done.1
  30.8 6.4 %all-to-all-done.1 = bf16[4,4,2,16,128]{4,3,2,1,0:T(8,128)(2,1)S(1)} async-done(((bf16[4,4,2,16,128]{4,3,2,1,0:T(8,128)(2,1)}), bf16[4,4,2,16,128]{4,3,2,1,0:T(8,128)(2,1)S(1)}, u32[]{:S(2)}, u32[]{:S(2)}) %all-to-all-start.1) | async-done | bytes 131104 | tf_op jit(solution)/shard_map/all_to_all | solution.py:89
  37.2 0.2 fusion.19
  37.4 0.1 fusion.7
  37.5 0.3 fusion.3
  37.7 0.7 %copy.40 = bf16[1,4,8,16,128]{4,3,1,0,2:T(8,128)(2,1)} copy(bf16[1,4,8,16,128]{4,3,2,1,0:T(8,128)(2,1)S(1)} %bitcast.56) | data formatting | bytes 262144 | tf_op jit(solution)/shard_map/reshape | solution.py:110
  38.4 3.3 %all-to-all-start.3 = ((bf16[1,4,8,16,128]{4,3,1,0,2:T(8,128)(2,1)}), bf16[1,4,8,16,128]{4,3,1,0,2:T(8,128)(2,1)S(1)}, u32[]{:S(2)}, u32[]{:S(2)}) async-start(bf16[1,4,8,16,128]{4,3,1,0,2:T(8,128)(2,1)} %copy.40), calls=%async_computation.3 | async-start | bytes 262144 | tf_op jit(solution)/shard_map/all_to_all | solution.py:112
  41.7 0.0 collective-permute-done.2
  41.8 0.0 copy-done
  41.8 0.4 bitcast_reduce_fusion
  42.2 0.4 fusion.1
  42.6 0.5 %divide_convert_fusion = bf16[2,256,128]{1,2,0:T(8,128)(2,1)S(1)} fusion(f32[2,256]{1,0:T(2,128)S(1)} %get-tuple-element.11, bf16[2,1024,128]{1,2,0:T(8,128)(2,1)S(1)} %all_gather.3, f32[2,1024,256]{2,1,0:T(8,128)S(1)} %get-tuple-element.15, f32[2,256]{1,0:T(2,128)S(1)} %get-tuple-element.14, f32[2,256]{1,0:T(2,128)S(1)} %get-tuple-element.10), kind=kOutput, calls=%fused_computation.13 | convolution fusion | flops 135987200 | bytes 2758656 | tf_op jit(solution)/shard_map/frn,fnd->frd/dot_general | solution.py:38
  43.1 4.5 %all-to-all-done.3 = bf16[1,4,8,16,128]{4,3,1,0,2:T(8,128)(2,1)S(1)} async-done(((bf16[1,4,8,16,128]{4,3,1,0,2:T(8,128)(2,1)}), bf16[1,4,8,16,128]{4,3,1,0,2:T(8,128)(2,1)S(1)}, u32[]{:S(2)}, u32[]{:S(2)}) %all-to-all-start.3) | async-done | bytes 131104 | tf_op jit(solution)/shard_map/all_to_all | solution.py:112
  47.6 0.1 copy.43
  47.8 0.8 %copy.44 = bf16[2,256,256]{2,1,0:T(8,128)(2,1)} copy(bf16[2,256,256]{1,2,0:T(8,128)(2,1)S(1)} %pad_maximum_fusion) | data formatting | bytes 524288 | tf_op jit(solution)/shard_map/concatenate | solution.py:124
  (9 shorter events, 0.1 us)
Async XLA Ops:
  0.0 10.9 %slice-start = ((bf16[2,256,256]{2,1,0:T(8,128)(2,1)}), bf16[2,256,128]{2,1,0:T(8,128)(2,1)S(1)}, s32[]{:S(2)}) async-start(bf16[2,256,256]{2,1,0:T(8,128)(2,1)} %param.3), calls=%async_computation.4 | async-start | bytes 262144 | tf_op jit(solution)/shard_map/slice | solution.py:81
  1.7 12.4 %all-to-all-start.2 = ((bf16[4,4,2,16,128]{4,3,2,1,0:T(8,128)(2,1)}), bf16[4,4,2,16,128]{4,3,2,1,0:T(8,128)(2,1)S(1)}, u32[]{:S(2)}, u32[]{:S(2)}) async-start(bf16[4,4,2,16,128]{4,3,2,1,0:T(8,128)(2,1)} %copy.37), calls=%async_computation.2 | async-start | bytes 262144 | tf_op jit(solution)/shard_map/all_to_all | solution.py:90
  9.1 16.1 %collective-permute-start = (bf16[2,256,128]{2,1,0:T(8,128)(2,1)S(1)}, bf16[2,256,128]{2,1,0:T(8,128)(2,1)S(1)}, u32[]{:S(2)}, u32[]{:S(2)}) collective-permute-start(bf16[2,256,128]{2,1,0:T(8,128)(2,1)S(1)} %get-tuple-element.7), channel_id=1, source_target_pairs={{0,1},{1,2},{2,3},{3,0},{4,5},{5,6},{6,7},{7,4},{8,9},{9,10},{10,1... | collective-permute-start | bytes 393224 | tf_op jit(solution)/shard_map/ppermute | solution.py:18
  9.2 21.5 %collective-permute-start.1 = (bf16[2,256,128]{2,1,0:T(8,128)(2,1)S(1)}, bf16[2,256,128]{2,1,0:T(8,128)(2,1)S(1)}, u32[]{:S(2)}, u32[]{:S(2)}) collective-permute-start(bf16[2,256,128]{2,1,0:T(8,128)(2,1)S(1)} %get-tuple-element.7), channel_id=1, source_target_pairs={{0,3},{1,0},{2,1},{3,2},{4,7},{5,4},{6,5},{7,6},{8,11},{9,8},{10,9... | collective-permute-start | bytes 393224 | tf_op jit(solution)/shard_map/ppermute | solution.py:21
  14.1 11.5 %all-to-all-start = ((bf16[4,4,2,16,128]{4,3,2,1,0:T(8,128)(2,1)}), bf16[4,4,2,16,128]{4,3,2,1,0:T(8,128)(2,1)S(1)}, u32[]{:S(2)}, u32[]{:S(2)}) async-start(bf16[4,4,2,16,128]{4,3,2,1,0:T(8,128)(2,1)} %copy.33), calls=%async_computation | async-start | bytes 262144 | tf_op jit(solution)/shard_map/all_to_all | solution.py:86
  25.3 16.5 %copy-start = (bf16[2,256,256]{2,1,0:T(8,128)(2,1)S(1)}, bf16[2,256,256]{2,1,0:T(8,128)(2,1)}, u32[]{:S(2)}) copy-start(bf16[2,256,256]{2,1,0:T(8,128)(2,1)} %param.3) | copy-start | bytes 786436
  25.3 16.4 %collective-permute-start.2 = (bf16[2,256,128]{2,1,0:T(8,128)(2,1)S(1)}, bf16[2,256,128]{2,1,0:T(8,128)(2,1)S(1)}, u32[]{:S(2)}, u32[]{:S(2)}) collective-permute-start(bf16[2,256,128]{2,1,0:T(8,128)(2,1)S(1)} %collective-permute-done), channel_id=1, source_target_pairs={{0,1},{1,2},{2,3},{3,0},{4,5},{5,6},{6,7},{7,4},{8,9},{9,10},{10,1... | collective-permute-start | bytes 393224 | tf_op jit(solution)/shard_map/ppermute | solution.py:18
  25.6 11.5 %all-to-all-start.1 = ((bf16[4,4,2,16,128]{4,3,2,1,0:T(8,128)(2,1)}), bf16[4,4,2,16,128]{4,3,2,1,0:T(8,128)(2,1)S(1)}, u32[]{:S(2)}, u32[]{:S(2)}) async-start(bf16[4,4,2,16,128]{4,3,2,1,0:T(8,128)(2,1)} %copy.35), calls=%async_computation.1 | async-start | bytes 262144 | tf_op jit(solution)/shard_map/all_to_all | solution.py:89
  38.4 9.2 %all-to-all-start.3 = ((bf16[1,4,8,16,128]{4,3,1,0,2:T(8,128)(2,1)}), bf16[1,4,8,16,128]{4,3,1,0,2:T(8,128)(2,1)S(1)}, u32[]{:S(2)}, u32[]{:S(2)}) async-start(bf16[1,4,8,16,128]{4,3,1,0,2:T(8,128)(2,1)} %copy.40), calls=%async_computation.3 | async-start | bytes 262144 | tf_op jit(solution)/shard_map/all_to_all | solution.py:112
